TPU v7x, 32 devices: a whole 2x2x4 slice. The times are simulated.
32 devices in a mesh: reg: 16 (over z, x, core), lev: 2 (over y).
Axes of the slice: x: 2, y: 2, z: 4, core: 2. Of those that a mesh axis runs over, the one named last changes fastest.
Arguments:
- state_now: bfloat16 [24, 1280, 2560], P(None, 'reg', 'lev'), may hold values from -6 to 6
- dep_cell: int32 [8, 1280, 2560], P(None, 'reg', 'lev'), may hold values from 0 to 63, as said below
- weight_code: int32 [8, 1280, 2560], P(None, 'reg', 'lev'), may hold values from 0 to 288, as said below
- wave_speed: float32 [8], replicated, may hold values from 0.05 to 5
Outputs:
- state_next: bfloat16 [24, 1280, 2560], P(None, 'reg', 'lev')
Inputs may be any that keep to these rules, and one draw needn't show every extreme that they name: `dep_cell`: 2 * 4 (a + 4) + b + 4 with whole numbers a and b from -4 to 3; both ends of that range occur for a and for b. `weight_code`: 17 a + b with whole numbers a and b from 0 to 16.
All inputs are finite; a program needn't handle non-finite values.
Results may differ from a plain program's by a relative error of at most 0.0084.
Values may be sent and summed in bfloat16 or wider, within the bound.
A program may use at most 64 MiB of HBM per device.

v0:
```python
import math
import jax
import jax.numpy as jnp
from jax import lax
from jax.sharding import PartitionSpec as P

NLAT = 1280
NLON = 2560
MX = 640
MY = 640
FIELDS = 3
HALO = 4


def padded_2(block, sides, width):
    for axis, dim in sides:
        count = lax.axis_size(axis)
        forward = [(i, i + 1) for i in range(count - 1)]
        forward.append((count - 1, 0))
        backward = [(target, source) for source, target in forward]
        low = lax.ppermute(
            lax.slice_in_dim(block, block.shape[dim] - width, None, axis=dim), axis, forward
        )
        high = lax.ppermute(lax.slice_in_dim(block, 0, width, axis=dim), axis, backward)
        block = jnp.concatenate([low, block, high], axis=dim)
    return block


def wave_table(length, modes, offset, amount):
    position = offset + lax.iota(jnp.int32, amount)
    wavenum = lax.iota(jnp.int32, 2 * modes) % modes
    product = position[:, None] * wavenum[None, :] % length
    angles = product.astype(jnp.float32) * (2.0 * math.pi / length)
    cosine_part = lax.iota(jnp.int32, 2 * modes) < modes
    return jnp.where(cosine_part[None, :], jnp.cos(angles), jnp.sin(angles)).astype(jnp.bfloat16)


def implicit_solve(spectral, xindex, speeds):
    wave_x = xindex % MX
    wave_y = lax.iota(jnp.int32, 2 * MY) % MY
    kx_term = 2.0 * math.pi / NLON * wave_x.astype(jnp.float32)
    ky_term = 2.0 * math.pi / NLAT * wave_y.astype(jnp.float32)
    laplace = kx_term[:, None] ** 2 + ky_term[None, :] ** 2
    inside = wave_x[:, None] * wave_x[:, None] + wave_y[None, :] * wave_y[None, :] < MX * MY
    weight_x = jnp.where(wave_x == 0, 1.0, 2.0)
    weight_y = jnp.where(wave_y == 0, 1.0, 2.0)
    factor = jnp.where(inside, weight_x[:, None] * weight_y[None, :], 0.0).astype(jnp.float32)
    speed_sq = speeds[:, None, None]
    vorticity = spectral[:, 0]
    divergence = spectral[:, 1]
    pressure = spectral[:, 2]
    div_new = (divergence + laplace * pressure) / (1.0 + speed_sq * laplace)
    pres_new = pressure - speed_sq * div_new
    stacked = jnp.stack([vorticity, div_new, pres_new], axis=1)
    return (stacked * factor[None, None]).astype(jnp.bfloat16)


def shift_weights(cell_code, code_index):
    shift_row = cell_code // (2 * HALO) - HALO
    shift_col = cell_code % (2 * HALO) - HALO
    weight_row = (code_index // 17).astype(jnp.float32) / 16.0
    weight_col = (code_index % 17).astype(jnp.float32) / 16.0
    row_weights = []
    col_weights = []
    for offset in range(-HALO, HALO + 1):
        row_weights.append(
            jnp.where(shift_row == offset, 1.0 - weight_row, 0.0)
            + jnp.where(shift_row + 1 == offset, weight_row, 0.0)
        )
        col_weights.append(
            jnp.where(shift_col == offset, 1.0 - weight_col, 0.0)
            + jnp.where(shift_col + 1 == offset, weight_col, 0.0)
        )
    return (row_weights, col_weights)


def interpolate_local(padded, row_weights, col_weights):
    levels, rows_pad, cols_pad = padded.shape
    rows_here = rows_pad - 2 * HALO
    cols_here = cols_pad - 2 * HALO
    blended = jnp.zeros((levels, rows_here, cols_here), jnp.float32)
    for row_step in range(2 * HALO + 1):
        inner = jnp.zeros((levels, rows_here, cols_here), jnp.float32)
        for col_step in range(2 * HALO + 1):
            window = padded[:, row_step : row_step + rows_here, col_step : col_step + cols_here]
            inner = inner + col_weights[col_step] * window.astype(jnp.float32)
        blended = blended + row_weights[row_step] * inner
    return blended.astype(jnp.bfloat16)


def per_device(state_now, dep_cell, weight_code, wave_speed):
    stacked, rows_here, cols_here = state_now.shape
    levels = stacked // FIELDS
    col_first = lax.axis_index("lev") * cols_here
    grouped = state_now.reshape(levels, FIELDS, rows_here, cols_here)
    row_weights, col_weights = shift_weights(dep_cell, weight_code)
    passes = []
    for which_field in range(FIELDS):
        padded = padded_2(grouped[:, which_field], (("reg", 1), ("lev", 2)), HALO)
        passes.append(interpolate_local(padded, row_weights, col_weights))
    upstream = jnp.stack(passes, axis=1).reshape(stacked, rows_here, cols_here)
    lon_table = wave_table(NLON, MX, 0, NLON)
    full_rows = lax.all_to_all(upstream, "lev", split_axis=0, concat_axis=2, tiled=True)
    lon_sum = jnp.einsum("krj,jc->krc", full_rows, lon_table, preferred_element_type=jnp.float32)
    lon_coef = (lon_sum / NLON).astype(jnp.bfloat16)
    lat_table = wave_table(NLAT, MY, 0, NLAT)
    spectral = (
        jnp.einsum(
            "klc,ly->kcy",
            lax.all_to_all(lon_coef, "reg", split_axis=2, concat_axis=1, tiled=True),
            lat_table,
            preferred_element_type=jnp.float32,
        )
        / NLAT
    )
    share = spectral.shape[1]
    xindex = lax.axis_index("reg") * share + lax.iota(jnp.int32, share)
    level_count = spectral.shape[0] // FIELDS
    speeds = lax.dynamic_slice_in_dim(
        wave_speed, lax.axis_index("lev") * level_count, level_count, 0
    )
    solved = implicit_solve(spectral.reshape(level_count, FIELDS, share, 2 * MY), xindex, speeds)
    solved = solved.reshape(level_count * FIELDS, share, 2 * MY)
    back_lat = jnp.einsum(
        "kcy,ly->kcl", solved, lat_table, preferred_element_type=jnp.float32
    ).astype(jnp.bfloat16)
    back_coef = lax.all_to_all(back_lat, "reg", split_axis=2, concat_axis=1, tiled=True)
    own_table = wave_table(NLON, MX, col_first, cols_here)
    return jnp.einsum(
        "kcr,jc->krj",
        lax.all_gather(back_coef, "lev", axis=0, tiled=True),
        own_table,
        preferred_element_type=jnp.float32,
    ).astype(jnp.bfloat16)


def solution(mesh):
    placed = (P(None, "reg", "lev"), P(None, "reg", "lev"), P(None, "reg", "lev"), P())
    return jax.shard_map(
        per_device, mesh=mesh, in_specs=placed, out_specs=P(None, "reg", "lev"), check_vma=False
    )
```

profile of v0, /device:TPU:0, one launch (start us, length us, event | category | flops | bytes accessed | tf_op | source)
XLA Modules:
  0.0 738.9 jit_solution(3293429734263387196)
XLA Ops:
  44.9 75.1 %fusion.69 = bf16[8,1,80,1280]{3,2,0,1:T(8,128)(2,1)} fusion(bf16[8,88,1284]{2,1,0:T(8,128)(2,1)S(1)} %get-tuple-element.12, bf16[8,4,1280]{2,1,0:T(4,128)(2,1)S(1)} %collective-permute-done.1, bf16[8,80,1280]{2,1,0:T(8,128)(2,1)} %copy-done.4, bf16[8,88,1284]{2,1,0:T(8,128)(2,1)S(1)} %get-tuple-element.11, ...), kind=kLoop, calls=%fused_computation.152 | loop fusion | flops 333414400 | bytes 127959040 | tf_op jit(solution)/shard_map/stack | solution.py:101
  120.0 76.8 %fusion.70 = bf16[8,1,80,1280]{3,2,0,1:T(8,128)(2,1)} fusion(bf16[8,88,1284]{2,1,0:T(8,128)(2,1)S(1)} %get-tuple-element.16, bf16[8,4,1280]{2,1,0:T(4,128)(2,1)} %copy-done.8, bf16[8,80,1280]{2,1,0:T(8,128)(2,1)} %copy-done.3, bf16[8,88,1284]{2,1,0:T(8,128)(2,1)S(1)} %get-tuple-element.15, bf16[8,4,1280]{2,1,0:T(4,128)(2,1)} %copy-done.5, ...), kind=kLoop, calls=%fused_computation.153 | loop fusion | flops 333414400 | bytes 127959040 | tf_op jit(solution)/shard_map/stack | solution.py:101
  201.2 75.0 %fusion.71 = bf16[8,1,80,1280]{3,2,0,1:T(8,128)(2,1)} fusion(bf16[8,88,1284]{2,1,0:T(8,128)(2,1)S(1)} %get-tuple-element.20, bf16[8,4,1280]{2,1,0:T(4,128)(2,1)S(1)} %copy-done.7, bf16[8,80,1280]{2,1,0:T(8,128)(2,1)} %copy-done.2, bf16[8,88,1284]{2,1,0:T(8,128)(2,1)S(1)} %get-tuple-element.19, bf16[8,4,1280]{2,1,0:T(4,128)(2,1)S(1)} %collective-permute-done.8, ...), kind=kLoop, calls=%fused_computation.154 | loop fusion | flops 333414400 | bytes 127959040 | tf_op jit(solution)/shard_map/stack | solution.py:101
  281.7 6.3 all-to-all-start
  288.1 47.1 %all-to-all-done = bf16[24,80,1280]{2,1,0:T(8,128)(2,1)} async-done(((bf16[24,80,1280]{2,1,0:T(8,128)(2,1)}), bf16[24,80,1280]{2,1,0:T(8,128)(2,1)}, u32[]{:S(2)}, u32[]{:S(2)}) %all-to-all-start) | async-done | bytes 4915232 | tf_op jit(solution)/shard_map/all_to_all | solution.py:103
  338.0 58.4 %multiply_convert_fusion = bf16[12,80,1280]{2,1,0:T(8,128)(2,1)S(1)} fusion(bf16[12,80,2560]{2,1,0:T(8,128)(2,1)S(1)} %bitcast.85, s32[1280]{0:T(1024)S(1)} %add_select_fusion.7, pred[1280]{0:T(1024)(128)(4,1)S(1)} %iota_compare_fusion), kind=kOutput, calls=%fused_computation.36 | convolution fusion | flops 6329958400 | bytes 7379200 | tf_op jit(solution)/shard_map/krj,jc->krc/dot_general | solution.py:104
  396.4 5.9 copy.17
  402.3 9.9 %reshape.160 = bf16[16,2,38400]{2,1,0:T(2,128)(2,1)} reshape(bf16[1280,12,80]{2,1,0:T(8,128)(2,1)} %bitcast.79) | data formatting | bytes 4915200
  412.2 6.3 all-to-all-start.1
  418.9 46.9 %all-to-all-done.1 = bf16[16,2,38400]{2,1,0:T(2,128)(2,1)S(1)} async-done(((bf16[16,2,38400]{2,1,0:T(2,128)(2,1)}), bf16[16,2,38400]{2,1,0:T(2,128)(2,1)S(1)}, u32[]{:S(2)}, u32[]{:S(2)}) %all-to-all-start.1) | async-done | bytes 2457632 | tf_op jit(solution)/shard_map/all_to_all | solution.py:110
  465.8 9.3 %reshape.161 = bf16[1280,12,80]{2,1,0:T(8,128)(2,1)} reshape(bf16[16,2,38400]{2,1,0:T(2,128)(2,1)S(1)} %all-to-all-done.1) | data formatting | bytes 4915200
  475.1 6.9 copy.25
  482.1 6.1 all_to_all.46
  488.1 30.0 %convolution_multiply_fusion = f32[12,80,1280]{2,1,0:T(8,128)S(1)} fusion(bf16[12,1280,80]{1,2,0:T(8,128)(2,1)S(1)} %all_to_all.46, s32[1280]{0:T(1024)S(1)} %add_select_fusion.7, pred[1280]{0:T(1024)(128)(4,1)S(1)} %iota_compare_fusion), kind=kOutput, calls=%fused_computation.44 | convolution fusion | flops 3164979200 | bytes 7379200 | tf_op jit(solution)/shard_map/klc,ly->kcy/dot_general | solution.py:108
  519.6 30.3 %convolution_convert_fusion.1 = bf16[12,80,1280]{2,1,0:T(8,128)(2,1)S(1)} fusion(bf16[12,80,1280]{2,1,0:T(8,128)(2,1)S(1)} %fusion.23, s32[1280]{0:T(1024)S(1)} %add_select_fusion.7, pred[1280]{0:T(1024)(128)(4,1)S(1)} %iota_compare_fusion), kind=kOutput, calls=%fused_computation.46 | convolution fusion | flops 3164979200 | bytes 4921600 | tf_op jit(solution)/shard_map/kcy,ly->kcl/dot_general | solution.py:124
  549.9 5.7 copy.19
  555.6 8.8 %reshape.162 = bf16[16,2,38400]{2,1,0:T(2,128)(2,1)S(1)} reshape(bf16[1280,12,80]{2,1,0:T(8,128)(2,1)} %bitcast.80) | data formatting | bytes 4915200
  564.4 68.5 %all_to_all.54 = bf16[16,2,38400]{2,1,0:T(2,128)(2,1)} all-to-all(bf16[16,2,38400]{2,1,0:T(2,128)(2,1)S(1)} %reshape.162), channel_id=1, replica_groups=mesh['reg'=16,'lev'=2] {'reg'}, dimensions={0} | all-to-all | bytes 4915200 | tf_op jit(solution)/shard_map/all_to_all | solution.py:127
  633.0 10.7 %reshape.163 = bf16[1280,12,80]{2,1,0:T(8,128)(2,1)} reshape(bf16[16,2,38400]{2,1,0:T(2,128)(2,1)} %all_to_all.54) | data formatting | bytes 4915200
  643.7 6.9 copy.20
  650.6 7.1 all_to_all.50
  657.8 27.7 %fusion.109 = bf16[1280,1280,1]{1,0,2:T(8,128)(2,1)S(1)} fusion(s32[1280]{0:T(1024)S(1)} %iota_add_fusion, s32[1280]{0:T(1024)S(1)} %add_select_fusion.7, pred[1280]{0:T(1024)(128)(4,1)S(1)} %iota_compare_fusion), kind=kLoop, calls=%fused_computation.48.clone.clone.1 | loop fusion | flops 18022400 | bytes 3288320 | tf_op jit(solution)/shard_map/kcr,jc->krj/dot_general | solution.py:129
  685.5 36.1 %all-gather.2.cloned.1.call-done = bf16[24,1280,80]{1,2,0:T(8,128)(2,1)} async-done(((bf16[12,1280,80]{1,2,0:T(8,128)(2,1)}), bf16[24,1280,80]{1,2,0:T(8,128)(2,1)}) %all-gather.2.cloned.1.call-update) | async-done | bytes 4915216 | tf_op jit(solution)/shard_map/all_gather | solution.py:131
  721.7 9.9 %convolution_convert_fusion = bf16[24,80,1280]{2,1,0:T(8,128)(2,1)} fusion(bf16[24,1280,80]{1,2,0:T(8,128)(2,1)} %all-gather.2.cloned.1.call-done, bf16[1280,1280,1]{1,0,2:T(8,128)(2,1)S(1)} %fusion.109), kind=kOutput, calls=%fused_computation.31 | convolution fusion | flops 6293913600 | bytes 13107200 | tf_op jit(solution)/shard_map/kcr,jc->krj/dot_general | solution.py:129
  (73 shorter events, 52.7 us)
Async XLA Ops:
  9.3 20.2 %copy-start.2 = (bf16[8,80,1280]{2,1,0:T(8,128)(2,1)}, bf16[8,80,1280]{2,1,0:T(8,128)(2,1)S(1)}, u32[]{:S(2)}) copy-start(bf16[8,80,1280]{2,1,0:T(8,128)(2,1)S(1)} %get-tuple-element.9) | copy-start | bytes 4915204
  9.3 26.3 %copy-start.4 = (bf16[8,80,1280]{2,1,0:T(8,128)(2,1)}, bf16[8,80,1280]{2,1,0:T(8,128)(2,1)S(1)}, u32[]{:S(2)}) copy-start(bf16[8,80,1280]{2,1,0:T(8,128)(2,1)S(1)} %get-tuple-element.8) | copy-start | bytes 4915204
  9.3 33.2 %copy-start.3 = (bf16[8,80,1280]{2,1,0:T(8,128)(2,1)}, bf16[8,80,1280]{2,1,0:T(8,128)(2,1)S(1)}, u32[]{:S(2)}) copy-start(bf16[8,80,1280]{2,1,0:T(8,128)(2,1)S(1)} %get-tuple-element.10) | copy-start | bytes 4915204
  9.4 10.2 %collective-permute-start = (bf16[8,4,1280]{2,1,0:T(4,128)(2,1)S(1)}, bf16[8,4,1280]{2,1,0:T(4,128)(2,1)S(1)}, u32[]{:S(2)}, u32[]{:S(2)}) collective-permute-start(bf16[8,4,1280]{2,1,0:T(4,128)(2,1)S(1)} %get-tuple-element.23), channel_id=1, source_target_pairs={{0,2},{2,4},{4,6},{6,8},{8,10},{10,12},{12,14},{14,16},{16,18},{18... | collective-permute-start | bytes 245768 | tf_op jit(solution)/shard_map/ppermute | solution.py:21
  9.9 14.2 %collective-permute-start.1 = (bf16[8,4,1280]{2,1,0:T(4,128)(2,1)S(1)}, bf16[8,4,1280]{2,1,0:T(4,128)(2,1)S(1)}, u32[]{:S(2)}, u32[]{:S(2)}) collective-permute-start(bf16[8,4,1280]{2,1,0:T(4,128)(2,1)S(1)} %get-tuple-element.24), channel_id=1, source_target_pairs={{2,0},{4,2},{6,4},{8,6},{10,8},{12,10},{14,12},{16,14},{18,16},{20... | collective-permute-start | bytes 245768 | tf_op jit(solution)/shard_map/ppermute | solution.py:24
  15.0 11.2 %collective-permute-start.4 = (bf16[8,4,1280]{2,1,0:T(4,128)(2,1)S(1)}, bf16[8,4,1280]{2,1,0:T(4,128)(2,1)S(1)}, u32[]{:S(2)}, u32[]{:S(2)}) collective-permute-start(bf16[8,4,1280]{2,1,0:T(4,128)(2,1)S(1)} %get-tuple-element.25), channel_id=1, source_target_pairs={{0,2},{2,4},{4,6},{6,8},{8,10},{10,12},{12,14},{14,16},{16,18},{18... | collective-permute-start | bytes 245768 | tf_op jit(solution)/shard_map/ppermute | solution.py:21
  15.1 11.3 %collective-permute-start.5 = (bf16[8,4,1280]{2,1,0:T(4,128)(2,1)S(1)}, bf16[8,4,1280]{2,1,0:T(4,128)(2,1)S(1)}, u32[]{:S(2)}, u32[]{:S(2)}) collective-permute-start(bf16[8,4,1280]{2,1,0:T(4,128)(2,1)S(1)} %get-tuple-element.26), channel_id=1, source_target_pairs={{2,0},{4,2},{6,4},{8,6},{10,8},{12,10},{14,12},{16,14},{18,16},{20... | collective-permute-start | bytes 245768 | tf_op jit(solution)/shard_map/ppermute | solution.py:24
  19.6 8.9 %collective-permute-start.8 = (bf16[8,4,1280]{2,1,0:T(4,128)(2,1)S(1)}, bf16[8,4,1280]{2,1,0:T(4,128)(2,1)S(1)}, u32[]{:S(2)}, u32[]{:S(2)}) collective-permute-start(bf16[8,4,1280]{2,1,0:T(4,128)(2,1)S(1)} %get-tuple-element.27), channel_id=1, source_target_pairs={{0,2},{2,4},{4,6},{6,8},{8,10},{10,12},{12,14},{14,16},{16,18},{18... | collective-permute-start | bytes 245768 | tf_op jit(solution)/shard_map/ppermute | solution.py:21
  19.6 8.9 %collective-permute-start.9 = (bf16[8,4,1280]{2,1,0:T(4,128)(2,1)S(1)}, bf16[8,4,1280]{2,1,0:T(4,128)(2,1)S(1)}, u32[]{:S(2)}, u32[]{:S(2)}) collective-permute-start(bf16[8,4,1280]{2,1,0:T(4,128)(2,1)S(1)} %get-tuple-element.28), channel_id=1, source_target_pairs={{2,0},{4,2},{6,4},{8,6},{10,8},{12,10},{14,12},{16,14},{18,16},{20... | collective-permute-start | bytes 245768 | tf_op jit(solution)/shard_map/ppermute | solution.py:24
  24.2 7.6 %collective-permute-start.2 = (bf16[8,88,4]{2,1,0:T(8,128)(2,1)S(1)}, bf16[8,88,4]{2,1,0:T(8,128)(2,1)S(1)}, u32[]{:S(2)}, u32[]{:S(2)}) collective-permute-start(bf16[8,88,4]{2,1,0:T(8,128)(2,1)S(1)} %get-tuple-element.13), channel_id=1, source_target_pairs={{0,1},{1,0},{2,3},{3,2},{4,5},{5,4},{6,7},{7,6},{8,9},{9,8},{10,11... | collective-permute-start | bytes 16904 | tf_op jit(solution)/shard_map/ppermute | solution.py:21
  26.2 16.3 %copy-start.5 = (bf16[8,4,1280]{2,1,0:T(4,128)(2,1)}, bf16[8,4,1280]{2,1,0:T(4,128)(2,1)S(1)}, u32[]{:S(2)}) copy-start(bf16[8,4,1280]{2,1,0:T(4,128)(2,1)S(1)} %collective-permute-done.4) | copy-start | bytes 245764
  26.2 9.4 %collective-permute-start.3 = (bf16[8,88,4]{2,1,0:T(8,128)(2,1)S(1)}, bf16[8,88,4]{2,1,0:T(8,128)(2,1)S(1)}, u32[]{:S(2)}, u32[]{:S(2)}) collective-permute-start(bf16[8,88,4]{2,1,0:T(8,128)(2,1)S(1)} %get-tuple-element.14), channel_id=1, source_target_pairs={{1,0},{0,1},{3,2},{2,3},{5,4},{4,5},{7,6},{6,7},{9,8},{8,9},{11,10... | collective-permute-start | bytes 16904 | tf_op jit(solution)/shard_map/ppermute | solution.py:24
  26.3 16.2 %copy-start.8 = (bf16[8,4,1280]{2,1,0:T(4,128)(2,1)}, bf16[8,4,1280]{2,1,0:T(4,128)(2,1)S(1)}, u32[]{:S(2)}) copy-start(bf16[8,4,1280]{2,1,0:T(4,128)(2,1)S(1)} %collective-permute-done.5) | copy-start | bytes 245764
  26.5 13.0 %collective-permute-start.6 = (bf16[8,88,4]{2,1,0:T(8,128)(2,1)S(1)}, bf16[8,88,4]{2,1,0:T(8,128)(2,1)S(1)}, u32[]{:S(2)}, u32[]{:S(2)}) collective-permute-start(bf16[8,88,4]{2,1,0:T(8,128)(2,1)S(1)} %get-tuple-element.17), channel_id=1, source_target_pairs={{0,1},{1,0},{2,3},{3,2},{4,5},{5,4},{6,7},{7,6},{8,9},{9,8},{10,11... | collective-permute-start | bytes 16904 | tf_op jit(solution)/shard_map/ppermute | solution.py:21
  28.5 14.1 %collective-permute-start.7 = (bf16[8,88,4]{2,1,0:T(8,128)(2,1)S(1)}, bf16[8,88,4]{2,1,0:T(8,128)(2,1)S(1)}, u32[]{:S(2)}, u32[]{:S(2)}) collective-permute-start(bf16[8,88,4]{2,1,0:T(8,128)(2,1)S(1)} %get-tuple-element.18), channel_id=1, source_target_pairs={{1,0},{0,1},{3,2},{2,3},{5,4},{4,5},{7,6},{6,7},{9,8},{8,9},{11,10... | collective-permute-start | bytes 16904 | tf_op jit(solution)/shard_map/ppermute | solution.py:24
  28.6 5.1 copy-start.6
  29.5 167.4 %collective-permute-start.10 = (bf16[8,88,4]{2,1,0:T(8,128)(2,1)}, bf16[8,88,4]{2,1,0:T(8,128)(2,1)}, u32[]{:S(2)}, u32[]{:S(2)}) collective-permute-start(bf16[8,88,4]{2,1,0:T(8,128)(2,1)} %get-tuple-element.21), channel_id=1, source_target_pairs={{0,1},{1,0},{2,3},{3,2},{4,5},{5,4},{6,7},{7,6},{8,9},{9,8},{10,11... | collective-permute-start | bytes 16904 | tf_op jit(solution)/shard_map/ppermute | solution.py:21
  31.8 165.1 %collective-permute-start.11 = (bf16[8,88,4]{2,1,0:T(8,128)(2,1)}, bf16[8,88,4]{2,1,0:T(8,128)(2,1)}, u32[]{:S(2)}, u32[]{:S(2)}) collective-permute-start(bf16[8,88,4]{2,1,0:T(8,128)(2,1)} %get-tuple-element.22), channel_id=1, source_target_pairs={{1,0},{0,1},{3,2},{2,3},{5,4},{4,5},{7,6},{6,7},{9,8},{8,9},{11,10... | collective-permute-start | bytes 16904 | tf_op jit(solution)/shard_map/ppermute | solution.py:24
  37.9 6.9 copy-start
  120.0 76.9 %copy-start.7 = (bf16[8,4,1280]{2,1,0:T(4,128)(2,1)S(1)}, bf16[8,4,1280]{2,1,0:T(4,128)(2,1)}, u32[]{:S(2)}) copy-start(bf16[8,4,1280]{2,1,0:T(4,128)(2,1)} %copy-done.6) | copy-start | bytes 245764
  281.7 53.4 %all-to-all-start = ((bf16[24,80,1280]{2,1,0:T(8,128)(2,1)}), bf16[24,80,1280]{2,1,0:T(8,128)(2,1)}, u32[]{:S(2)}, u32[]{:S(2)}) async-start(bf16[24,80,1280]{2,1,0:T(8,128)(2,1)} %bitcast.81), calls=%async_computation | async-start | bytes 9830400 | tf_op jit(solution)/shard_map/all_to_all | solution.py:103
  412.2 6.3 copy-start.9
  412.2 53.7 %all-to-all-start.1 = ((bf16[16,2,38400]{2,1,0:T(2,128)(2,1)}), bf16[16,2,38400]{2,1,0:T(2,128)(2,1)S(1)}, u32[]{:S(2)}, u32[]{:S(2)}) async-start(bf16[16,2,38400]{2,1,0:T(2,128)(2,1)} %reshape.160), calls=%async_computation.1 | async-start | bytes 4915200 | tf_op jit(solution)/shard_map/all_to_all | solution.py:110
  418.5 303.2 %all-gather.2.cloned.1.call-start = ((), (), s32[]{:S(2)}) async-start(), calls=%async_computation.3 | async-start | bytes 7372800 | tf_op jit(solution)/shard_map/all_gather | solution.py:131
  (1 other events, 4.3 us)
Sparse Core Ops, SparseCore 0:
  657.9 63.7 all-gather.1
where the time goes:
time: 747 us; the launch traced here: 739 us
  other arithmetic  269 us (36%)
  waiting for transfers between devices  137 us (18%)
  matrix products  129 us (17%)
  local copies, waits for them, and re-layouts  85.9 us (11%)
  blocking collectives  68.5 us (9%)
  starting transfers between devices  35.2 us (5%)
  between operations  14.2 us (2%)
    another operation x4, other arithmetic, per_device(): upstream = jnp.stack(passes, axis=1).reshape(stacked, rows_here, cols_here)  230 us
    all_to_all x1, blocking collectives, per_device(): lax.all_to_all(back_lat, 'reg', split_axis=2, concat_axis=1, tiled=True)  68.5 us
    dot_general x1, matrix products, per_device(): jnp.einsum('krj,jc->krc', full_rows, lon_table, preferred_element_type=jn...  58.4 us
    all_to_all x1, waiting for transfers between devices, per_device(): lax.all_to_all(upstream, 'lev', split_axis=0, concat_axis=2, tiled=True)  47.1 us
    all_to_all x1, waiting for transfers between devices, per_device(): lax.all_to_all(lon_coef, 'reg', split_axis=2, concat_axis=1, tiled=True)  46.9 us
    unnamed x24, local copies, waits for them, and re-layouts  38.7 us
    all_gather x1, waiting for transfers between devices, per_device(): lax.all_gather(back_coef, 'lev', axis=0, tiled=True)  36.1 us
    dot_general x1, matrix products, per_device(): jnp.einsum('kcy,ly->kcl', solved, lat_table, preferred_element_type=jnp.f...  30.3 us
  transfers between devices with their start and end apart: 15, of which 7 were waited for; matrix products, arithmetic and copies ran while one was open for 25% of the time, Pallas kernels for 0%

commit v1 on v0

--- a/solution.py
+++ b/solution.py
@@ -10,6 +10,18 @@
 MY = 640
 FIELDS = 3
 HALO = 4
+
+
+def collect(x, axis, dim):
+    ways, here = (lax.axis_size(axis), lax.axis_index(axis))
+    grown, reach = (x, 1)
+    while reach < ways:
+        theirs = lax.ppermute(grown, axis, [(d, d ^ reach) for d in range(ways)])
+        mine_first = jnp.concatenate([grown, theirs], axis=dim)
+        theirs_first = jnp.concatenate([theirs, grown], axis=dim)
+        grown = jnp.where(here & reach == 0, mine_first, theirs_first)
+        reach = 2 * reach
+    return grown
 
 
 def padded_2(block, sides, width):
@@ -127,10 +139,7 @@
     back_coef = lax.all_to_all(back_lat, "reg", split_axis=2, concat_axis=1, tiled=True)
     own_table = wave_table(NLON, MX, col_first, cols_here)
     return jnp.einsum(
-        "kcr,jc->krj",
-        lax.all_gather(back_coef, "lev", axis=0, tiled=True),
-        own_table,
-        preferred_element_type=jnp.float32,
+        "kcr,jc->krj", collect(back_coef, "lev", 0), own_table, preferred_element_type=jnp.float32
     ).astype(jnp.bfloat16)
 
 

time: 747 us -> 725 us (0.971)
  between operations: 14.2 us -> 0.81 us
  waiting for transfers between devices: 137 us -> 129 us
    all_gather x1 -> x0, waiting for transfers between devices: 36.1 us -> none  [per_device(): lax.all_gather(back_coef, 'lev', axis=0, tiled=True)]
    ppermute x0 -> x1, waiting for transfers between devices: none -> 28.4 us  [collect(): theirs = lax.ppermute(grown, axis, [(d, d ^ reach) for d in range(ways)])]
  transfers between devices with their start and end apart: 15 -> 15, of which waited for: 7 -> 7; matrix products, arithmetic and copies ran while one was open for 25% -> 26% of each run, Pallas kernels for 0% -> 0%
where the time goes in v1:
time: 725 us; the launch traced here: 717 us
  other arithmetic  269 us (37%)
  waiting for transfers between devices  129 us (18%)
  matrix products  129 us (18%)
  local copies, waits for them, and re-layouts  84.8 us (12%)
  blocking collectives  68.5 us (9%)
  starting transfers between devices  35.2 us (5%)
    another operation x4, other arithmetic, per_device(): upstream = jnp.stack(passes, axis=1).reshape(stacked, rows_here, cols_here)  229 us
    all_to_all x1, blocking collectives, per_device(): lax.all_to_all(back_lat, 'reg', split_axis=2, concat_axis=1, tiled=True)  68.5 us
    dot_general x1, matrix products, per_device(): jnp.einsum('krj,jc->krc', full_rows, lon_table, preferred_element_type=jn...  58.4 us
    all_to_all x1, waiting for transfers between devices, per_device(): lax.all_to_all(upstream, 'lev', split_axis=0, concat_axis=2, tiled=True)  47.1 us
    all_to_all x1, waiting for transfers between devices, per_device(): lax.all_to_all(lon_coef, 'reg', split_axis=2, concat_axis=1, tiled=True)  47 us
    unnamed x24, local copies, waits for them, and re-layouts  38.7 us
    dot_general x1, matrix products, per_device(): jnp.einsum('kcy,ly->kcl', solved, lat_table, preferred_element_type=jnp.f...  30.3 us
    dot_general x1, matrix products, per_device(): jnp.einsum('klc,ly->kcy', lax.all_to_all(lon_coef, 'reg', split_axis=2, c...  30 us
  transfers between devices with their start and end apart: 15, of which 7 were waited for; matrix products, arithmetic and copies ran while one was open for 26% of the time, Pallas kernels for 0%

profile of v1, /device:TPU:0, one launch (start us, length us, event | category | flops | bytes accessed | tf_op | source)
XLA Modules:
  0.0 716.6 jit_solution(4747754501743831405)
XLA Ops:
  38.3 75.1 %fusion.75 = bf16[8,1,80,1280]{3,2,0,1:T(8,128)(2,1)} fusion(bf16[8,88,1284]{2,1,0:T(8,128)(2,1)S(1)} %get-tuple-element.12, bf16[8,4,1280]{2,1,0:T(4,128)(2,1)S(1)} %collective-permute-done.1, bf16[8,80,1280]{2,1,0:T(8,128)(2,1)} %copy-done.4, bf16[8,88,1284]{2,1,0:T(8,128)(2,1)S(1)} %get-tuple-element.11, ...), kind=kLoop, calls=%fused_computation.159 | loop fusion | flops 333414400 | bytes 127959040 | tf_op jit(solution)/shard_map/stack | solution.py:113
  113.5 76.1 %fusion.76 = bf16[8,1,80,1280]{3,2,0,1:T(8,128)(2,1)} fusion(bf16[8,88,1284]{2,1,0:T(8,128)(2,1)S(1)} %get-tuple-element.16, bf16[8,4,1280]{2,1,0:T(4,128)(2,1)} %copy-done.8, bf16[8,80,1280]{2,1,0:T(8,128)(2,1)} %copy-done.3, bf16[8,88,1284]{2,1,0:T(8,128)(2,1)S(1)} %get-tuple-element.15, bf16[8,4,1280]{2,1,0:T(4,128)(2,1)} %copy-done.5, ...), kind=kLoop, calls=%fused_computation.160 | loop fusion | flops 333414400 | bytes 127959040 | tf_op jit(solution)/shard_map/stack | solution.py:113
  193.9 75.0 %fusion.77 = bf16[8,1,80,1280]{3,2,0,1:T(8,128)(2,1)} fusion(bf16[8,88,1284]{2,1,0:T(8,128)(2,1)S(1)} %get-tuple-element.20, bf16[8,4,1280]{2,1,0:T(4,128)(2,1)S(1)} %copy-done.7, bf16[8,80,1280]{2,1,0:T(8,128)(2,1)} %copy-done.2, bf16[8,88,1284]{2,1,0:T(8,128)(2,1)S(1)} %get-tuple-element.19, bf16[8,4,1280]{2,1,0:T(4,128)(2,1)S(1)} %collective-permute-done.8, ...), kind=kLoop, calls=%fused_computation.161 | loop fusion | flops 333414400 | bytes 127959040 | tf_op jit(solution)/shard_map/stack | solution.py:113
  274.5 6.3 all-to-all-start
  280.8 47.1 %all-to-all-done = bf16[24,80,1280]{2,1,0:T(8,128)(2,1)} async-done(((bf16[24,80,1280]{2,1,0:T(8,128)(2,1)}), bf16[24,80,1280]{2,1,0:T(8,128)(2,1)}, u32[]{:S(2)}, u32[]{:S(2)}) %all-to-all-start) | async-done | bytes 4915232 | tf_op jit(solution)/shard_map/all_to_all | solution.py:115
  330.8 58.4 %multiply_convert_fusion = bf16[12,80,1280]{2,1,0:T(8,128)(2,1)S(1)} fusion(bf16[12,80,2560]{2,1,0:T(8,128)(2,1)S(1)} %bitcast.84, s32[1280]{0:T(1024)S(1)} %add_select_fusion.7, pred[1280]{0:T(1024)(128)(4,1)S(1)} %iota_compare_fusion), kind=kOutput, calls=%fused_computation.42 | convolution fusion | flops 6329958400 | bytes 7379200 | tf_op jit(solution)/shard_map/krj,jc->krc/dot_general | solution.py:116
  389.2 5.9 copy.17
  395.1 9.9 %reshape.160 = bf16[16,2,38400]{2,1,0:T(2,128)(2,1)} reshape(bf16[1280,12,80]{2,1,0:T(8,128)(2,1)} %bitcast.78) | data formatting | bytes 4915200
  405.0 6.3 all-to-all-start.1
  411.7 47.0 %all-to-all-done.1 = bf16[16,2,38400]{2,1,0:T(2,128)(2,1)S(1)} async-done(((bf16[16,2,38400]{2,1,0:T(2,128)(2,1)}), bf16[16,2,38400]{2,1,0:T(2,128)(2,1)S(1)}, u32[]{:S(2)}, u32[]{:S(2)}) %all-to-all-start.1) | async-done | bytes 2457632 | tf_op jit(solution)/shard_map/all_to_all | solution.py:122
  458.6 9.3 %reshape.161 = bf16[1280,12,80]{2,1,0:T(8,128)(2,1)} reshape(bf16[16,2,38400]{2,1,0:T(2,128)(2,1)S(1)} %all-to-all-done.1) | data formatting | bytes 4915200
  467.9 6.9 copy.25
  474.8 6.1 all_to_all.46
  480.9 30.0 %convolution_multiply_fusion = f32[12,80,1280]{2,1,0:T(8,128)S(1)} fusion(bf16[12,1280,80]{1,2,0:T(8,128)(2,1)S(1)} %all_to_all.46, s32[1280]{0:T(1024)S(1)} %add_select_fusion.7, pred[1280]{0:T(1024)(128)(4,1)S(1)} %iota_compare_fusion), kind=kOutput, calls=%fused_computation.51 | convolution fusion | flops 3164979200 | bytes 7379200 | tf_op jit(solution)/shard_map/klc,ly->kcy/dot_general | solution.py:120
  512.4 30.3 %convolution_convert_fusion.1 = bf16[12,80,1280]{2,1,0:T(8,128)(2,1)S(1)} fusion(bf16[12,80,1280]{2,1,0:T(8,128)(2,1)S(1)} %fusion.28, s32[1280]{0:T(1024)S(1)} %add_select_fusion.7, pred[1280]{0:T(1024)(128)(4,1)S(1)} %iota_compare_fusion), kind=kOutput, calls=%fused_computation.53 | convolution fusion | flops 3164979200 | bytes 4921600 | tf_op jit(solution)/shard_map/kcy,ly->kcl/dot_general | solution.py:136
  542.7 5.7 copy.19
  548.4 8.8 %reshape.162 = bf16[16,2,38400]{2,1,0:T(2,128)(2,1)S(1)} reshape(bf16[1280,12,80]{2,1,0:T(8,128)(2,1)} %bitcast.79) | data formatting | bytes 4915200
  557.2 68.5 %all_to_all.54 = bf16[16,2,38400]{2,1,0:T(2,128)(2,1)} all-to-all(bf16[16,2,38400]{2,1,0:T(2,128)(2,1)S(1)} %reshape.162), channel_id=1, replica_groups=mesh['reg'=16,'lev'=2] {'reg'}, dimensions={0} | all-to-all | bytes 4915200 | tf_op jit(solution)/shard_map/all_to_all | solution.py:139
  625.7 10.7 %reshape.163 = bf16[1280,12,80]{2,1,0:T(8,128)(2,1)} reshape(bf16[16,2,38400]{2,1,0:T(2,128)(2,1)} %all_to_all.54) | data formatting | bytes 4915200
  636.5 6.9 copy.20
  643.4 6.1 all_to_all.50
  649.6 27.7 %fusion.115 = bf16[1280,1280,1]{1,0,2:T(8,128)(2,1)S(1)} fusion(s32[1280]{0:T(1024)S(1)} %iota_add_fusion, s32[1280]{0:T(1024)S(1)} %add_select_fusion.7, pred[1280]{0:T(1024)(128)(4,1)S(1)} %iota_compare_fusion), kind=kLoop, calls=%fused_computation.55.clone.clone.2 | loop fusion | flops 18022400 | bytes 3288320 | tf_op jit(solution)/shard_map/kcr,jc->krj/dot_general | solution.py:141
  677.3 28.4 %collective-permute-done.12 = bf16[12,1280,80]{1,2,0:T(8,128)(2,1)} collective-permute-done((bf16[12,1280,80]{1,2,0:T(8,128)(2,1)S(1)}, bf16[12,1280,80]{1,2,0:T(8,128)(2,1)}, u32[]{:S(2)}, u32[]{:S(2)}) %collective-permute-start.12) | collective-permute-done | bytes 2457632 | tf_op jit(solution)/shard_map/ppermute | solution.py:19
  705.7 10.5 %convolution_convert_fusion = bf16[24,80,1280]{2,1,0:T(8,128)(2,1)} fusion(bf16[12,1280,80]{1,2,0:T(8,128)(2,1)} %collective-permute-done.12, bf16[12,1280,80]{1,2,0:T(8,128)(2,1)S(1)} %all_to_all.50, pred[]{:T(512)S(6)} %eq.142, bf16[1280,1280,1]{1,0,2:T(8,128)(2,1)S(1)} %fusion.115), kind=kOutput, calls=%fused_computation.31 | convolution fusion | flops 6301286400 | bytes 13107201 | tf_op jit(solution)/shard_map/kcr,jc->krj/dot_general | solution.py:141
  (72 shorter events, 52.7 us)
Async XLA Ops:
  2.7 20.2 %copy-start.2 = (bf16[8,80,1280]{2,1,0:T(8,128)(2,1)}, bf16[8,80,1280]{2,1,0:T(8,128)(2,1)S(1)}, u32[]{:S(2)}) copy-start(bf16[8,80,1280]{2,1,0:T(8,128)(2,1)S(1)} %get-tuple-element.9) | copy-start | bytes 4915204
  2.8 26.3 %copy-start.4 = (bf16[8,80,1280]{2,1,0:T(8,128)(2,1)}, bf16[8,80,1280]{2,1,0:T(8,128)(2,1)S(1)}, u32[]{:S(2)}) copy-start(bf16[8,80,1280]{2,1,0:T(8,128)(2,1)S(1)} %get-tuple-element.8) | copy-start | bytes 4915204
  2.8 33.2 %copy-start.3 = (bf16[8,80,1280]{2,1,0:T(8,128)(2,1)}, bf16[8,80,1280]{2,1,0:T(8,128)(2,1)S(1)}, u32[]{:S(2)}) copy-start(bf16[8,80,1280]{2,1,0:T(8,128)(2,1)S(1)} %get-tuple-element.10) | copy-start | bytes 4915204
  2.9 10.2 %collective-permute-start = (bf16[8,4,1280]{2,1,0:T(4,128)(2,1)S(1)}, bf16[8,4,1280]{2,1,0:T(4,128)(2,1)S(1)}, u32[]{:S(2)}, u32[]{:S(2)}) collective-permute-start(bf16[8,4,1280]{2,1,0:T(4,128)(2,1)S(1)} %get-tuple-element.23), channel_id=1, source_target_pairs={{0,2},{2,4},{4,6},{6,8},{8,10},{10,12},{12,14},{14,16},{16,18},{18... | collective-permute-start | bytes 245768 | tf_op jit(solution)/shard_map/ppermute | solution.py:33
  3.4 14.2 %collective-permute-start.1 = (bf16[8,4,1280]{2,1,0:T(4,128)(2,1)S(1)}, bf16[8,4,1280]{2,1,0:T(4,128)(2,1)S(1)}, u32[]{:S(2)}, u32[]{:S(2)}) collective-permute-start(bf16[8,4,1280]{2,1,0:T(4,128)(2,1)S(1)} %get-tuple-element.24), channel_id=1, source_target_pairs={{2,0},{4,2},{6,4},{8,6},{10,8},{12,10},{14,12},{16,14},{18,16},{20... | collective-permute-start | bytes 245768 | tf_op jit(solution)/shard_map/ppermute | solution.py:36
  8.5 11.2 %collective-permute-start.4 = (bf16[8,4,1280]{2,1,0:T(4,128)(2,1)S(1)}, bf16[8,4,1280]{2,1,0:T(4,128)(2,1)S(1)}, u32[]{:S(2)}, u32[]{:S(2)}) collective-permute-start(bf16[8,4,1280]{2,1,0:T(4,128)(2,1)S(1)} %get-tuple-element.25), channel_id=1, source_target_pairs={{0,2},{2,4},{4,6},{6,8},{8,10},{10,12},{12,14},{14,16},{16,18},{18... | collective-permute-start | bytes 245768 | tf_op jit(solution)/shard_map/ppermute | solution.py:33
  8.5 11.3 %collective-permute-start.5 = (bf16[8,4,1280]{2,1,0:T(4,128)(2,1)S(1)}, bf16[8,4,1280]{2,1,0:T(4,128)(2,1)S(1)}, u32[]{:S(2)}, u32[]{:S(2)}) collective-permute-start(bf16[8,4,1280]{2,1,0:T(4,128)(2,1)S(1)} %get-tuple-element.26), channel_id=1, source_target_pairs={{2,0},{4,2},{6,4},{8,6},{10,8},{12,10},{14,12},{16,14},{18,16},{20... | collective-permute-start | bytes 245768 | tf_op jit(solution)/shard_map/ppermute | solution.py:36
  13.0 8.9 %collective-permute-start.8 = (bf16[8,4,1280]{2,1,0:T(4,128)(2,1)S(1)}, bf16[8,4,1280]{2,1,0:T(4,128)(2,1)S(1)}, u32[]{:S(2)}, u32[]{:S(2)}) collective-permute-start(bf16[8,4,1280]{2,1,0:T(4,128)(2,1)S(1)} %get-tuple-element.27), channel_id=1, source_target_pairs={{0,2},{2,4},{4,6},{6,8},{8,10},{10,12},{12,14},{14,16},{16,18},{18... | collective-permute-start | bytes 245768 | tf_op jit(solution)/shard_map/ppermute | solution.py:33
  13.1 8.9 %collective-permute-start.9 = (bf16[8,4,1280]{2,1,0:T(4,128)(2,1)S(1)}, bf16[8,4,1280]{2,1,0:T(4,128)(2,1)S(1)}, u32[]{:S(2)}, u32[]{:S(2)}) collective-permute-start(bf16[8,4,1280]{2,1,0:T(4,128)(2,1)S(1)} %get-tuple-element.28), channel_id=1, source_target_pairs={{2,0},{4,2},{6,4},{8,6},{10,8},{12,10},{14,12},{16,14},{18,16},{20... | collective-permute-start | bytes 245768 | tf_op jit(solution)/shard_map/ppermute | solution.py:36
  17.7 7.6 %collective-permute-start.2 = (bf16[8,88,4]{2,1,0:T(8,128)(2,1)S(1)}, bf16[8,88,4]{2,1,0:T(8,128)(2,1)S(1)}, u32[]{:S(2)}, u32[]{:S(2)}) collective-permute-start(bf16[8,88,4]{2,1,0:T(8,128)(2,1)S(1)} %get-tuple-element.13), channel_id=1, source_target_pairs={{0,1},{1,0},{2,3},{3,2},{4,5},{5,4},{6,7},{7,6},{8,9},{9,8},{10,11... | collective-permute-start | bytes 16904 | tf_op jit(solution)/shard_map/ppermute | solution.py:33
  19.7 16.3 %copy-start.5 = (bf16[8,4,1280]{2,1,0:T(4,128)(2,1)}, bf16[8,4,1280]{2,1,0:T(4,128)(2,1)S(1)}, u32[]{:S(2)}) copy-start(bf16[8,4,1280]{2,1,0:T(4,128)(2,1)S(1)} %collective-permute-done.4) | copy-start | bytes 245764
  19.7 9.4 %collective-permute-start.3 = (bf16[8,88,4]{2,1,0:T(8,128)(2,1)S(1)}, bf16[8,88,4]{2,1,0:T(8,128)(2,1)S(1)}, u32[]{:S(2)}, u32[]{:S(2)}) collective-permute-start(bf16[8,88,4]{2,1,0:T(8,128)(2,1)S(1)} %get-tuple-element.14), channel_id=1, source_target_pairs={{1,0},{0,1},{3,2},{2,3},{5,4},{4,5},{7,6},{6,7},{9,8},{8,9},{11,10... | collective-permute-start | bytes 16904 | tf_op jit(solution)/shard_map/ppermute | solution.py:36
  19.8 16.2 %copy-start.8 = (bf16[8,4,1280]{2,1,0:T(4,128)(2,1)}, bf16[8,4,1280]{2,1,0:T(4,128)(2,1)S(1)}, u32[]{:S(2)}) copy-start(bf16[8,4,1280]{2,1,0:T(4,128)(2,1)S(1)} %collective-permute-done.5) | copy-start | bytes 245764
  19.9 13.0 %collective-permute-start.6 = (bf16[8,88,4]{2,1,0:T(8,128)(2,1)S(1)}, bf16[8,88,4]{2,1,0:T(8,128)(2,1)S(1)}, u32[]{:S(2)}, u32[]{:S(2)}) collective-permute-start(bf16[8,88,4]{2,1,0:T(8,128)(2,1)S(1)} %get-tuple-element.17), channel_id=1, source_target_pairs={{0,1},{1,0},{2,3},{3,2},{4,5},{5,4},{6,7},{7,6},{8,9},{9,8},{10,11... | collective-permute-start | bytes 16904 | tf_op jit(solution)/shard_map/ppermute | solution.py:33
  21.9 14.1 %collective-permute-start.7 = (bf16[8,88,4]{2,1,0:T(8,128)(2,1)S(1)}, bf16[8,88,4]{2,1,0:T(8,128)(2,1)S(1)}, u32[]{:S(2)}, u32[]{:S(2)}) collective-permute-start(bf16[8,88,4]{2,1,0:T(8,128)(2,1)S(1)} %get-tuple-element.18), channel_id=1, source_target_pairs={{1,0},{0,1},{3,2},{2,3},{5,4},{4,5},{7,6},{6,7},{9,8},{8,9},{11,10... | collective-permute-start | bytes 16904 | tf_op jit(solution)/shard_map/ppermute | solution.py:36
  22.0 5.1 copy-start.6
  22.9 166.7 %collective-permute-start.10 = (bf16[8,88,4]{2,1,0:T(8,128)(2,1)}, bf16[8,88,4]{2,1,0:T(8,128)(2,1)}, u32[]{:S(2)}, u32[]{:S(2)}) collective-permute-start(bf16[8,88,4]{2,1,0:T(8,128)(2,1)} %get-tuple-element.21), channel_id=1, source_target_pairs={{0,1},{1,0},{2,3},{3,2},{4,5},{5,4},{6,7},{7,6},{8,9},{9,8},{10,11... | collective-permute-start | bytes 16904 | tf_op jit(solution)/shard_map/ppermute | solution.py:33
  25.2 164.4 %collective-permute-start.11 = (bf16[8,88,4]{2,1,0:T(8,128)(2,1)}, bf16[8,88,4]{2,1,0:T(8,128)(2,1)}, u32[]{:S(2)}, u32[]{:S(2)}) collective-permute-start(bf16[8,88,4]{2,1,0:T(8,128)(2,1)} %get-tuple-element.22), channel_id=1, source_target_pairs={{1,0},{0,1},{3,2},{2,3},{5,4},{4,5},{7,6},{6,7},{9,8},{8,9},{11,10... | collective-permute-start | bytes 16904 | tf_op jit(solution)/shard_map/ppermute | solution.py:36
  31.4 6.9 copy-start
  113.5 76.2 %copy-start.7 = (bf16[8,4,1280]{2,1,0:T(4,128)(2,1)S(1)}, bf16[8,4,1280]{2,1,0:T(4,128)(2,1)}, u32[]{:S(2)}) copy-start(bf16[8,4,1280]{2,1,0:T(4,128)(2,1)} %copy-done.6) | copy-start | bytes 245764
  274.5 53.4 %all-to-all-start = ((bf16[24,80,1280]{2,1,0:T(8,128)(2,1)}), bf16[24,80,1280]{2,1,0:T(8,128)(2,1)}, u32[]{:S(2)}, u32[]{:S(2)}) async-start(bf16[24,80,1280]{2,1,0:T(8,128)(2,1)} %bitcast.80), calls=%async_computation | async-start | bytes 9830400 | tf_op jit(solution)/shard_map/all_to_all | solution.py:115
  405.0 6.3 copy-start.9
  405.0 53.7 %all-to-all-start.1 = ((bf16[16,2,38400]{2,1,0:T(2,128)(2,1)}), bf16[16,2,38400]{2,1,0:T(2,128)(2,1)S(1)}, u32[]{:S(2)}, u32[]{:S(2)}) async-start(bf16[16,2,38400]{2,1,0:T(2,128)(2,1)} %reshape.160), calls=%async_computation.1 | async-start | bytes 4915200 | tf_op jit(solution)/shard_map/all_to_all | solution.py:122
  649.5 56.2 %collective-permute-start.12 = (bf16[12,1280,80]{1,2,0:T(8,128)(2,1)S(1)}, bf16[12,1280,80]{1,2,0:T(8,128)(2,1)}, u32[]{:S(2)}, u32[]{:S(2)}) collective-permute-start(bf16[12,1280,80]{1,2,0:T(8,128)(2,1)S(1)} %all_to_all.50), channel_id=1, source_target_pairs={{0,1},{1,0},{2,3},{3,2},{4,5},{5,4},{6,7},{7,6},{8,9},{9,8},{10,11... | collective-permute-start | bytes 7372808 | tf_op jit(solution)/shard_map/ppermute | solution.py:19
  (1 other events, 4.3 us)
